TPU v7x, 32 devices: a whole 2x2x4 slice. The times are simulated.
32 devices in a mesh: grid: 8 (over y, x, core), pt: 4 (over z).
Axes of the slice: x: 2, y: 2, z: 4, core: 2. Of those that a mesh axis runs over, the one named last changes fastest.
Arguments:
- orbitals: bfloat16 [2048, 4096], P('grid'), may hold values from -0.875 to 0.875
- point_index: int32 [2048], P('pt'), may hold values from 0 to 4095, as said below
- factor_panels: float32 [2048, 1024], P('pt'), as said below
Outputs:
- solved: float32 [4096, 2048], P('grid', 'pt')
Inputs may be any that keep to these rules, and one draw needn't show every extreme that they name: `point_index`: all entries are different; 0 and 4095 are always among them. `factor_panels`: lower triangular in its global row and column indices, diagonal between 1.5 and 3.
All inputs are finite; a program needn't handle non-finite values.
Results may differ from a plain program's by a relative error of at most 0.0018.
Values may be sent and summed in bfloat16 or wider, within the bound.
A program may use at most 64 MiB of HBM per device.

v0:
```python
import jax
import jax.numpy as jnp
from jax import lax
from jax.sharding import PartitionSpec as P


def spread(x, axis, root):
    mine = lax.axis_index(axis) == root
    return lax.psum(jnp.where(mine, x, jnp.zeros_like(x)), axis)


def solve_panel(factor, targets):
    return lax.linalg.triangular_solve(
        factor, targets, left_side=False, lower=True, transpose_a=True
    )


def apply_factor(panel_round, factor):
    upper_part = factor.astype(jnp.bfloat16)
    lower_part = (factor - upper_part.astype(jnp.float32)).astype(jnp.bfloat16)
    dims = (((1,), (1,)), ((), ()))
    high_term = lax.dot_general(panel_round, upper_part, dims, preferred_element_type=jnp.float32)
    low_term = lax.dot_general(panel_round, lower_part, dims, preferred_element_type=jnp.float32)
    return high_term + low_term


def on_device(orbitals, point_index, factor_panels):
    own_bands, grid_rows = orbitals.shape
    grid_count = lax.axis_size("grid")
    rows_here = grid_rows // grid_count
    panel_cols = point_index.shape[0]
    at_points = jnp.take(orbitals, point_index, axis=1)
    point_orbs = lax.all_gather(at_points, "grid", axis=0, tiled=True)
    blocked = orbitals.reshape(own_bands, grid_count, rows_here)
    inner_sums = lax.dot_general(
        lax.all_to_all(blocked, "grid", split_axis=1, concat_axis=0, tiled=True)[:, 0, :],
        point_orbs,
        (((0,), (0,)), ((), ())),
        preferred_element_type=jnp.float32,
    )
    products = inner_sums * inner_sums
    rank_pt = lax.axis_index("pt")
    factor_first = factor_panels[:, 0:panel_cols]
    factor_second = factor_panels[:, panel_cols : 2 * panel_cols]
    first_solved = lax.cond(
        rank_pt == 0, lambda: solve_panel(factor_first, products), lambda: jnp.zeros_like(products)
    )
    first_round = spread(first_solved.astype(jnp.bfloat16), "pt", 0)
    left_over = lax.cond(
        rank_pt > 0, lambda: products - apply_factor(first_round, factor_first), lambda: products
    )
    second_solved = lax.cond(
        rank_pt == 1,
        lambda: solve_panel(factor_second, left_over),
        lambda: jnp.zeros_like(left_over),
    )
    second_round = spread(second_solved.astype(jnp.bfloat16), "pt", 1)
    trailing = lax.cond(
        rank_pt > 1,
        lambda: left_over - apply_factor(second_round, factor_second),
        lambda: left_over,
    )
    return jnp.where(rank_pt == 0, first_solved, jnp.where(rank_pt == 1, second_solved, trailing))


def solution(mesh):
    in_specs = (P("grid", None), P("pt"), P("pt", None))
    out_specs = P("grid", "pt")
    return jax.shard_map(
        on_device, mesh=mesh, in_specs=in_specs, out_specs=out_specs, check_vma=False
    )
```

profile of v0, /device:TPU:0, one launch (start us, length us, event | category | flops | bytes accessed | tf_op | source)
XLA Modules:
  0.0 292.4 jit_solution(4851775570383524236)
XLA Ops:
  6.5 0.0 all-gather.2.cloned.1.call-start
  6.5 0.7 compare_select_fusion
  7.2 0.7 compare_and_fusion
  7.9 4.1 %copy.26 = bf16[256,4096]{0,1:T(8,128)(2,1)} copy(bf16[256,4096]{1,0:T(8,128)(2,1)} %param.13) | data formatting | bytes 4194304 | tf_op args[0]
  12.0 3.4 %gather_fusion = bf16[512,256]{1,0:T(8,128)(2,1)S(1)} fusion(bf16[256,4096]{0,1:T(8,128)(2,1)} %copy.26, s32[1024]{0:T(1024)S(1)} %pad_clamp_fusion), kind=kCustom, calls=%fused_computation | custom fusion | bytes 526336 | tf_op jit(solution)/shard_map/jit(_take)/gather | solution.py:32
  15.4 0.8 select_bitcast_fusion
  16.3 0.0 all-gather.2.cloned.1.call-update
  16.3 5.2 %all-to-all-start = ((bf16[256,8,512]{0,2,1:T(8,128)(2,1)}), bf16[256,8,512]{0,2,1:T(8,128)(2,1)}, u32[]{:S(2)}, u32[]{:S(2)}) async-start(bf16[256,8,512]{0,2,1:T(8,128)(2,1)} %bitcast.13), calls=%async_computation | async-start | bytes 4194304 | tf_op jit(solution)/shard_map/all_to_all | solution.py:36
  21.5 0.0 all-reduce.3.cloned.1.call-start
  21.6 1.7 fusion.53
  23.3 31.2 %all-to-all-done = bf16[256,8,512]{0,2,1:T(8,128)(2,1)} async-done(((bf16[256,8,512]{0,2,1:T(8,128)(2,1)}), bf16[256,8,512]{0,2,1:T(8,128)(2,1)}, u32[]{:S(2)}, u32[]{:S(2)}) %all-to-all-start) | async-done | bytes 2097184 | tf_op jit(solution)/shard_map/all_to_all | solution.py:36
  54.5 3.9 %copy.28 = bf16[8,256,1,512]{3,1,0,2:T(8,128)(2,1)} copy(bf16[8,256,1,512]{1,3,0,2:T(8,128)(2,1)} %bitcast.15) | data formatting | bytes 4194304 | tf_op jit(solution)/shard_map/all_to_all | solution.py:36
  58.4 0.0 all-gather.2.cloned.1.call-done
  58.5 3.5 %fusion.50 = f32[512,512]{0,1:T(8,128)S(1)} fusion(bf16[2048,512]{0,1:T(8,128)(2,1)} %all-gather.2.cloned.1.call-done, bf16[2048,512]{1,0:T(8,128)(2,1)} %bitcast.89), kind=kOutput, calls=%fused_computation.80 | convolution fusion | flops 1074003968 | bytes 5242880 | tf_op jit(solution)/shard_map/dot_general | solution.py:35
  62.0 71.8 %conditional.4 = (f32[512,512]{1,0:T(8,128)}, bf16[512,512]{1,0:T(8,128)(2,1)}) conditional(s32[]{:T(128)} %convert_element_type.42, () %tuple.38, (f32[512,512]{1,0:T(8,128)S(1)}, f32[512,512]{0,1:T(8,128)S(1)}) %tuple.39), branch_computations={%region_0.1_spmd, %region_1.3_spmd} | conditional | flops 1010761728 | bytes 25428344 | solution.py:45
  62.0 1.1 fusion.10
  63.1 11.3 %while.4 = (s32[]{:T(128)}, f32[512,512]{1,0:T(8,128)}, s32[4,2]{0,1:T(2,128)S(1)}, f32[4,128,128]{2,1,0:T(8,128)S(1)}, s32[]{:T(128)}) while((s32[]{:T(128)}, f32[512,512]{1,0:T(8,128)}, s32[4,2]{0,1:T(2,128)S(1)}, f32[4,128,128]{2,1,0:T(8,128)S(1)}, s32[]{:T(128)}) %tuple.92), condition=%wide.while_cond, body=%wide.while_body.sunk | while | flops 2 | bytes 131181 | solution.py:13
  63.1 0.1 constant_dynamic-slice_fusion.5
  63.2 0.5 fusion.71
  63.8 2.2 bitcast_dynamic-update-slice_fusion.5
  66.0 0.1 constant_dynamic-slice_fusion.5
  66.0 0.5 fusion.71
  66.6 2.2 bitcast_dynamic-update-slice_fusion.5
  68.8 0.1 constant_dynamic-slice_fusion.5
  68.9 0.5 fusion.71
  69.4 2.2 bitcast_dynamic-update-slice_fusion.5
  71.6 0.1 constant_dynamic-slice_fusion.5
  71.7 0.5 fusion.71
  72.3 2.1 bitcast_dynamic-update-slice_fusion.5
  74.4 39.9 %custom-call.4 = f32[4,128,128]{1,2,0:T(8,128)} custom-call(f32[4,128,128]{2,1,0:T(8,128)S(1)} %get-tuple-element.70), custom_call_target="InvertDiagBlocksLowerTriangular" | custom-call | tf_op jit(solution)/shard_map/cond/branch_1_fun/triangular_solve/custom-call.1 | solution.py:13
  114.4 1.3 copy.29
  115.7 1.5 fusion.19
  117.2 1.6 convolution_subtract_fusion.1
  118.8 1.3 fusion.25
  120.0 0.0 copy-start.1
  120.0 0.0 copy-done.2
  120.0 2.0 convolution_subtract_fusion
  122.1 0.0 copy-done.7
  122.1 0.4 fusion.24
  122.5 0.0 copy-start.3
  122.5 2.5 convolution_subtract_fusion.2
  125.0 0.4 fusion.23
  125.4 0.0 copy-done.1
  125.4 0.0 copy-done.3
  125.4 0.0 copy-start.5
  125.5 0.7 copy-done.5
  126.2 0.9 fusion.29
  127.0 2.0 copy.41
  129.1 2.2 pad_maximum_fusion
  131.2 2.5 copy.39
  133.8 1.9 broadcast_select_fusion.1
  135.7 0.0 all-reduce.3.cloned.1.call-update
  135.7 0.0 all-reduce.5.cloned.1.call-start
  135.7 35.0 %all-reduce.3.cloned.1.call-done = bf16[512,512]{1,0:T(8,128)(2,1)} async-done(((bf16[512,512]{1,0:T(8,128)(2,1)}), bf16[512,512]{1,0:T(8,128)(2,1)}) %all-reduce.3.cloned.1.call-update) | async-done | bytes 524304 | tf_op jit(solution)/shard_map/psum | solution.py:9
  170.8 2.8 conditional.5
  170.8 1.0 copy-done
  171.8 1.6 copy.42
  173.6 2.0 conditional.6
  173.6 1.1 broadcast.31.clone
  174.7 0.8 broadcast.32.clone
  175.6 0.8 broadcast_select_fusion
  176.4 0.0 all-reduce.5.cloned.1.call-update
  176.4 107.0 %all-reduce.5.cloned.1.call-done = bf16[512,512]{1,0:T(8,128)(2,1)} async-done(((bf16[512,512]{1,0:T(8,128)(2,1)}), bf16[512,512]{1,0:T(8,128)(2,1)}) %all-reduce.5.cloned.1.call-update) | async-done | bytes 524304 | tf_op jit(solution)/shard_map/psum | solution.py:9
  283.4 2.5 select_select_fusion
  (8 shorter events, 0.0 us)
Async XLA Ops:
  6.5 51.9 %all-gather.2.cloned.1.call-start = ((), (), s32[]{:S(2)}) async-start(), calls=%async_computation.1 | async-start | bytes 2359296 | tf_op jit(solution)/shard_map/all_gather | solution.py:33
  16.3 38.2 %all-to-all-start = ((bf16[256,8,512]{0,2,1:T(8,128)(2,1)}), bf16[256,8,512]{0,2,1:T(8,128)(2,1)}, u32[]{:S(2)}, u32[]{:S(2)}) async-start(bf16[256,8,512]{0,2,1:T(8,128)(2,1)} %bitcast.13), calls=%async_computation | async-start | bytes 4194304 | tf_op jit(solution)/shard_map/all_to_all | solution.py:36
  21.5 149.3 %all-reduce.3.cloned.1.call-start = ((), (), s32[]{:S(2)}) async-start(), calls=%async_computation.2 | async-start | bytes 1048576 | tf_op jit(solution)/shard_map/psum | solution.py:9
  115.7 4.4 %copy-start.2 = (f32[512,512]{1,0:T(8,128)S(1)}, f32[512,512]{1,0:T(8,128)}, u32[]{:S(2)}) copy-start(f32[512,512]{1,0:T(8,128)} %copy.29) | copy-start | bytes 3145732 | tf_op jit(solution)/shard_map/cond
  115.7 6.4 %copy-start.7 = (f32[4,128,128]{1,2,0:T(8,128)S(1)}, f32[4,128,128]{1,2,0:T(8,128)}, u32[]{:S(2)}) copy-start(f32[4,128,128]{1,2,0:T(8,128)} %custom-call.4) | copy-start | bytes 786436 | tf_op jit(solution)/shard_map/cond
  120.0 5.4 %copy-start.1 = (f32[512,128]{0,1:T(8,128)}, f32[512,128]{0,1:T(8,128)S(1)}, u32[]{:S(2)}) copy-start(f32[512,128]{0,1:T(8,128)S(1)} %fusion.25) | copy-start | bytes 786436 | tf_op jit(solution)/shard_map/cond
  122.5 2.9 %copy-start.3 = (f32[512,128]{0,1:T(8,128)}, f32[512,128]{0,1:T(8,128)S(1)}, u32[]{:S(2)}) copy-start(f32[512,128]{0,1:T(8,128)S(1)} %fusion.24) | copy-start | bytes 786436 | tf_op jit(solution)/shard_map/cond
  125.4 0.7 copy-start.5
  135.7 147.7 %all-reduce.5.cloned.1.call-start = ((), (), s32[]{:S(2)}) async-start(), calls=%async_computation.3 | async-start | bytes 1048576 | tf_op jit(solution)/shard_map/psum | solution.py:9
  170.8 1.0 copy-start
Sparse Core Ops, SparseCore 0:
  16.4 42.0 all-gather.1
  135.8 34.9 all-reduce.2
  176.5 106.7 all-reduce.4
where the time goes:
time: 293 us; the launch traced here: 292 us
  waiting for transfers between devices  173 us (59%)
  other arithmetic  51.6 us (18%)
  local copies, waits for them, and re-layouts  35.5 us (12%)
  between operations  13.2 us (5%)
  matrix products  13.1 us (4%)
  starting transfers between devices  5.29 us (2%)
    psum x2, waiting for transfers between devices, spread(): return lax.psum(jnp.where(mine, x, jnp.zeros_like(x)), axis)  142 us
    another operation x5, other arithmetic, solve_panel(): lax.linalg.triangular_solve(factor, targets, left_side=False, lower=True,...  43.3 us
    all_to_all x1, waiting for transfers between devices, on_device(): lax.all_to_all(blocked, 'grid', split_axis=1, concat_axis=0, tiled=True)  31.2 us
    another operation x12, local copies, waits for them, and re-layouts, solve_panel(): lax.linalg.triangular_solve(factor, targets, left_side=False, lower=True,...  11.2 us
    another operation x7, matrix products, solve_panel(): lax.linalg.triangular_solve(factor, targets, left_side=False, lower=True,...  9.67 us
  transfers between devices with their start and end apart: 4, of which 3 were waited for; matrix products, arithmetic and copies ran while one was open for 2% of the time, Pallas kernels for 0%

commit v1 on v0

--- a/solution.py
+++ b/solution.py
@@ -2,6 +2,13 @@
 import jax.numpy as jnp
 from jax import lax
 from jax.sharding import PartitionSpec as P
+
+
+def _load_cards(inner_x, ax_name):
+    last = lax.axis_size(ax_name)
+    arr_out = jnp.split(inner_x, last, 1)
+    upper = lax.all_to_all(jnp.stack(arr_out, axis=0), ax_name, concat_axis=0, split_axis=0)
+    return jnp.concatenate(upper, 0)
 
 
 def spread(x, axis, root):
@@ -33,7 +40,7 @@
     point_orbs = lax.all_gather(at_points, "grid", axis=0, tiled=True)
     blocked = orbitals.reshape(own_bands, grid_count, rows_here)
     inner_sums = lax.dot_general(
-        lax.all_to_all(blocked, "grid", split_axis=1, concat_axis=0, tiled=True)[:, 0, :],
+        _load_cards(blocked, "grid")[:, 0, :],
         point_orbs,
         (((0,), (0,)), ((), ())),
         preferred_element_type=jnp.float32,

time: 293 us -> 292 us (level)
    unnamed x1 -> x8, local copies, waits for them, and re-layouts: 4.08 us -> 8.36 us
  transfers between devices with their start and end apart: 4 -> 4, of which waited for: 3 -> 3; matrix products, arithmetic and copies ran while one was open for 2% -> 4% of each run, Pallas kernels for 0% -> 0%
where the time goes in v1:
time: 292 us
  waiting for transfers between devices  173 us (59%)
  other arithmetic  51.6 us (18%)
  local copies, waits for them, and re-layouts  35.5 us (12%)
  between operations  13.2 us (5%)
  matrix products  12.9 us (4%)
  starting transfers between devices  5.28 us (2%)
    psum x2, waiting for transfers between devices, spread(): return lax.psum(jnp.where(mine, x, jnp.zeros_like(x)), axis)  141 us
    another operation x5, other arithmetic, solve_panel(): lax.linalg.triangular_solve(factor, targets, left_side=False, lower=True,...  43.2 us
    all_to_all x1, waiting for transfers between devices, _load_cards(): lax.all_to_all(jnp.stack(arr_out, axis=0), ax_name, concat_axis=0, split_...  32.1 us
    another operation x12, local copies, waits for them, and re-layouts, solve_panel(): lax.linalg.triangular_solve(factor, targets, left_side=False, lower=True,...  11.5 us
    another operation x7, matrix products, solve_panel(): lax.linalg.triangular_solve(factor, targets, left_side=False, lower=True,...  9.36 us
    unnamed x8, local copies, waits for them, and re-layouts  8.36 us
  transfers between devices with their start and end apart: 4, of which 3 were waited for; matrix products, arithmetic and copies ran while one was open for 4% of the time, Pallas kernels for 0%

profile of v1, /device:TPU:0, one launch (start us, length us, event | category | flops | bytes accessed | tf_op | source)
XLA Modules:
  0.0 291.6 jit_solution(16674518785787383356)
XLA Ops:
  6.5 0.0 all-gather.2.cloned.1.call-start
  6.5 0.7 compare_select_fusion
  7.2 0.7 compare_and_fusion
  7.9 3.3 %copy.37 = bf16[256,4096]{0,1:T(8,128)(2,1)S(1)} copy(bf16[256,4096]{1,0:T(8,128)(2,1)} %param.13) | data formatting | bytes 4194304 | tf_op args[0]
  11.2 2.0 gather_fusion
  13.2 0.8 select_bitcast_fusion
  14.0 0.0 all-gather.2.cloned.1.call-update
  14.0 0.7 fusion.57
  14.8 0.7 fusion.56
  15.5 0.7 fusion.55
  16.2 0.7 fusion.54
  16.9 0.7 fusion.53
  17.7 0.7 fusion.52
  18.4 0.7 fusion.51
  19.1 0.7 fusion.50
  19.8 5.2 %all-to-all-start = ((bf16[8,256,1,512]{1,3,2,0:T(8,128)(2,1)}), bf16[8,256,1,512]{1,3,2,0:T(8,128)(2,1)}, u32[]{:S(2)}, u32[]{:S(2)}) async-start(bf16[8,256,1,512]{1,3,2,0:T(8,128)(2,1)} %fusion.50), calls=%async_computation | async-start | bytes 4194304 | tf_op jit(solution)/shard_map/all_to_all | solution.py:10
  25.0 0.0 all-reduce.3.cloned.1.call-start
  25.1 1.7 fusion.60
  26.8 32.1 %all-to-all-done = bf16[8,256,1,512]{1,3,2,0:T(8,128)(2,1)} async-done(((bf16[8,256,1,512]{1,3,2,0:T(8,128)(2,1)}), bf16[8,256,1,512]{1,3,2,0:T(8,128)(2,1)}, u32[]{:S(2)}, u32[]{:S(2)}) %all-to-all-start) | async-done | bytes 2097184 | tf_op jit(solution)/shard_map/all_to_all | solution.py:10
  58.9 3.9 %copy.40 = bf16[8,256,1,512]{3,1,0,2:T(8,128)(2,1)} copy(bf16[8,256,1,512]{1,3,2,0:T(8,128)(2,1)} %all-to-all-done) | data formatting | bytes 4194304 | tf_op jit(solution)/shard_map/all_to_all | solution.py:10
  62.8 3.5 %convolution_multiply_fusion = f32[512,512]{1,0:T(8,128)S(1)} fusion(bf16[2048,512]{1,0:T(8,128)(2,1)} %bitcast.124, bf16[2048,512]{0,1:T(8,128)(2,1)} %all-gather.2.cloned.1.call-done), kind=kOutput, calls=%fused_computation.79 | convolution fusion | flops 1074003968 | bytes 5242880 | tf_op jit(solution)/shard_map/dot_general | solution.py:42
  66.4 70.5 %conditional.4 = (f32[512,512]{1,0:T(8,128)}, bf16[512,512]{1,0:T(8,128)(2,1)}) conditional(s32[]{:T(128)} %convert_element_type.42, () %tuple.38, (f32[512,512]{1,0:T(8,128)S(1)}, f32[512,512]{1,0:T(8,128)S(1)}) %tuple.39), branch_computations={%region_0.1_spmd, %region_1.3_spmd} | conditional | flops 1010761728 | bytes 19136860 | solution.py:52
  66.4 1.1 fusion.10
  67.5 11.6 %while.4 = (s32[]{:T(128)}, f32[512,512]{1,0:T(8,128)}, s32[4,2]{0,1:T(2,128)S(1)}, f32[4,128,128]{2,1,0:T(8,128)S(1)}, s32[]{:T(128)}) while((s32[]{:T(128)}, f32[512,512]{1,0:T(8,128)}, s32[4,2]{0,1:T(2,128)S(1)}, f32[4,128,128]{2,1,0:T(8,128)S(1)}, s32[]{:T(128)}) %tuple.85), condition=%wide.while_cond, body=%wide.while_body.sunk | while | flops 2 | bytes 131181 | solution.py:20
  67.5 0.1 constant_dynamic-slice_fusion.5
  67.6 0.6 fusion.78
  68.1 2.2 bitcast_dynamic-update-slice_fusion.5
  70.4 0.1 constant_dynamic-slice_fusion.5
  70.5 0.6 fusion.78
  71.1 2.2 bitcast_dynamic-update-slice_fusion.5
  73.3 0.1 constant_dynamic-slice_fusion.5
  73.4 0.6 fusion.78
  74.0 2.2 bitcast_dynamic-update-slice_fusion.5
  76.2 0.1 constant_dynamic-slice_fusion.5
  76.3 0.6 fusion.78
  76.9 2.2 bitcast_dynamic-update-slice_fusion.5
  79.1 39.9 %custom-call.4 = f32[4,128,128]{1,2,0:T(8,128)} custom-call(f32[4,128,128]{2,1,0:T(8,128)S(1)} %get-tuple-element.70), custom_call_target="InvertDiagBlocksLowerTriangular" | custom-call | tf_op jit(solution)/shard_map/cond/branch_1_fun/triangular_solve/custom-call.1 | solution.py:20
  119.0 1.3 fusion.19
  120.4 1.4 convolution_subtract_fusion.1
  121.8 1.3 fusion.25
  123.1 0.0 copy-start
  123.1 2.0 convolution_subtract_fusion
  125.1 0.0 copy-done.6
  125.1 0.4 fusion.24
  125.5 0.0 copy-start.1
  125.5 2.5 convolution_subtract_fusion.2
  128.1 0.4 fusion.23
  128.5 0.0 copy-done
  128.5 0.7 copy-done.3
  129.2 0.9 fusion.29
  130.1 2.1 copy.52
  132.1 2.2 pad_maximum_fusion
  134.3 2.5 copy.50
  136.8 1.9 broadcast_select_fusion.1
  138.7 0.0 all-reduce.3.cloned.1.call-update
  138.8 0.0 all-reduce.5.cloned.1.call-start
  138.8 35.2 %all-reduce.3.cloned.1.call-done = bf16[512,512]{1,0:T(8,128)(2,1)} async-done(((bf16[512,512]{1,0:T(8,128)(2,1)}), bf16[512,512]{1,0:T(8,128)(2,1)}) %all-reduce.3.cloned.1.call-update) | async-done | bytes 524304 | tf_op jit(solution)/shard_map/psum | solution.py:16
  174.0 2.0 conditional.6
  174.0 1.1 broadcast.31.clone
  175.2 0.8 broadcast.32.clone
  176.0 0.9 broadcast_select_fusion
  176.9 0.0 all-reduce.5.cloned.1.call-update
  176.9 105.6 %all-reduce.5.cloned.1.call-done = bf16[512,512]{1,0:T(8,128)(2,1)} async-done(((bf16[512,512]{1,0:T(8,128)(2,1)}), bf16[512,512]{1,0:T(8,128)(2,1)}) %all-reduce.5.cloned.1.call-update) | async-done | bytes 524304 | tf_op jit(solution)/shard_map/psum | solution.py:16
  282.5 2.5 select_select_fusion
  (10 shorter events, 0.0 us)
Async XLA Ops:
  6.5 56.3 %all-gather.2.cloned.1.call-start = ((), (), s32[]{:S(2)}) async-start(), calls=%async_computation.1 | async-start | bytes 2359296 | tf_op jit(solution)/shard_map/all_gather | solution.py:40
  19.8 39.1 %all-to-all-start = ((bf16[8,256,1,512]{1,3,2,0:T(8,128)(2,1)}), bf16[8,256,1,512]{1,3,2,0:T(8,128)(2,1)}, u32[]{:S(2)}, u32[]{:S(2)}) async-start(bf16[8,256,1,512]{1,3,2,0:T(8,128)(2,1)} %fusion.50), calls=%async_computation | async-start | bytes 4194304 | tf_op jit(solution)/shard_map/all_to_all | solution.py:10
  25.0 149.0 %all-reduce.3.cloned.1.call-start = ((), (), s32[]{:S(2)}) async-start(), calls=%async_computation.2 | async-start | bytes 1048576 | tf_op jit(solution)/shard_map/psum | solution.py:16
  119.0 6.1 %copy-start.6 = (f32[4,128,128]{1,2,0:T(8,128)S(1)}, f32[4,128,128]{1,2,0:T(8,128)}, u32[]{:S(2)}) copy-start(f32[4,128,128]{1,2,0:T(8,128)} %custom-call.4) | copy-start | bytes 786436 | tf_op jit(solution)/shard_map/cond
  123.1 5.4 %copy-start = (f32[512,128]{0,1:T(8,128)}, f32[512,128]{0,1:T(8,128)S(1)}, u32[]{:S(2)}) copy-start(f32[512,128]{0,1:T(8,128)S(1)} %fusion.25) | copy-start | bytes 786436 | tf_op jit(solution)/shard_map/cond
  125.5 3.0 %copy-start.1 = (f32[512,128]{0,1:T(8,128)}, f32[512,128]{0,1:T(8,128)S(1)}, u32[]{:S(2)}) copy-start(f32[512,128]{0,1:T(8,128)S(1)} %fusion.24) | copy-start | bytes 786436 | tf_op jit(solution)/shard_map/cond
  128.5 0.7 copy-start.3
  138.8 143.7 %all-reduce.5.cloned.1.call-start = ((), (), s32[]{:S(2)}) async-start(), calls=%async_computation.3 | async-start | bytes 1048576 | tf_op jit(solution)/shard_map/psum | solution.py:16
Sparse Core Ops, SparseCore 0:
  14.1 42.8 all-gather.1
  138.9 35.1 all-reduce.2
  177.0 105.4 all-reduce.4
